TPU v7x, 32 devices: a whole 2x2x4 slice. The times are simulated.
32 devices in a mesh: tp: 4 (over y, x), grp: 8 (over z, core).
Axes of the slice: x: 2, y: 2, z: 4, core: 2. Of those that a mesh axis runs over, the one named last changes fastest.
Arguments:
- embeds: bfloat16 [2, 32, 8192], P(None, 'grp'), may hold values from -6 to 6
- ssm_state: bfloat16 [2, 32, 128, 64, 128], P(None, 'grp', 'tp'), may hold values from -2 to 2
- conv_state: bfloat16 [2, 32, 3, 8192], P(None, 'grp', None, 'tp'), may hold values from -6 to 6
- norm_gain: float32 [2, 8192], replicated, may hold values from 0.25 to 1.75
- in_weight: bfloat16 [2, 8192, 2, 8192], P(None, 'grp', None, 'tp'), may hold values from -0.0625 to 0.0625
- group_weight: bfloat16 [2, 8192, 384], P(None, 'grp'), may hold values from -0.03125 to 0.03125
- dt_bias: float32 [2, 128], P(None, 'tp'), may hold values from -2 to 1
- a_log: float32 [2, 128], P(None, 'tp'), may hold values from -1.5 to 1.5
- skip_gain: float32 [2, 128], P(None, 'tp'), may hold values from 0.5 to 1.5
- conv_weight: float32 [2, 4, 8192], P(None, None, 'tp'), may hold values from -3 to 3
- conv_bias: float32 [2, 8192], P(None, 'tp'), may hold values from -2 to 2
- out_weight: bfloat16 [2, 8192, 8192], P(None, 'tp', 'grp'), may hold values from -0.0625 to 0.0625
- leave_row: int32 [8], P('grp'), may hold values from 0 to 3
- arrive_from: int32 [8], P('grp'), may hold values from 0 to 7, as said below
Outputs:
- out_hidden: bfloat16 [2, 32, 8192], P(None, 'grp', 'tp')
Inputs may be any that keep to these rules, and one draw needn't show every extreme that they name: Every group appears exactly once in arrive_from: each group's leaving row fills exactly one freed slot.
All inputs are finite; a program needn't handle non-finite values.
Results may differ from a plain program's by a relative error of at most 0.02.
Values may be sent and summed in bfloat16 or wider, within the bound.
A program may use at most 128 MiB of HBM per device.

v0:
```python
import jax
import jax.numpy as jnp
from jax import lax
from jax.sharding import PartitionSpec as P


def local(
    embeds,
    ssm_state,
    conv_state,
    norm_gain,
    in_weight,
    group_weight,
    dt_bias,
    a_log,
    skip_gain,
    conv_weight,
    conv_bias,
    out_weight,
    leave_row,
    arrive_from,
):
    groups = lax.axis_size("grp")
    parts = lax.axis_size("tp")
    part_index = lax.axis_index("tp")
    steps = embeds.shape[0]
    row_dev = embeds.shape[1]
    model_width = embeds.shape[2]
    block_width = model_width // groups
    part_width = model_width // parts
    layers = ssm_state.shape[0]
    heads_dev = ssm_state.shape[2]
    head_dim = ssm_state.shape[3]
    state_dim = ssm_state.shape[4]
    channels = in_weight.shape[3]
    taps_count = conv_weight.shape[1]
    state_list = [ssm_state[i] for i in range(layers)]
    conv_list = [conv_state[i] for i in range(layers)]
    leaving = leave_row[0]
    anchor = arrive_from[0]

    def pick(carry, piece):
        count = piece[0].shape[0]
        hits = jnp.arange(count, dtype=jnp.int32) == anchor
        picked = []
        for total, member in zip(carry, piece):
            mask = hits.reshape((count,) + (1,) * (member.ndim - 1))
            picked.append(jnp.sum(jnp.where(mask, member, jnp.zeros_like(member)), axis=0))
        return tuple(picked)

    def leaving_rows():
        own_state = jnp.stack(
            [lax.dynamic_index_in_dim(s_arr, leaving, 0, False) for s_arr in state_list]
        )
        own_conv = jnp.stack(
            [lax.dynamic_index_in_dim(c_arr, leaving, 0, False) for c_arr in conv_list]
        )
        return (own_state, own_conv)

    def store_rows(got_state, got_conv):
        for i in range(layers):
            state_list[i] = lax.dynamic_update_index_in_dim(state_list[i], got_state[i], leaving, 0)
            conv_list[i] = lax.dynamic_update_index_in_dim(conv_list[i], got_conv[i], leaving, 0)

    def migrate_all():
        own_state, own_conv = leaving_rows()
        start_pair = (
            jnp.zeros(own_state.shape, jnp.bfloat16),
            jnp.zeros(own_conv.shape, jnp.bfloat16),
        )
        got_state, got_conv = pick(
            start_pair,
            (
                lax.all_gather(own_state[None], "grp", axis=0, tiled=True),
                lax.all_gather(own_conv[None], "grp", axis=0, tiled=True),
            ),
        )
        store_rows(got_state, got_conv)

    def migrate(layer):
        if layer == 0:
            migrate_all()

    def mixer(normed_block, layer):
        w_cols = in_weight[layer].reshape(block_width, 2 * channels)
        w_group = group_weight[layer]
        first = jnp.dot(normed_block, w_cols, preferred_element_type=jnp.float32)
        second = jnp.dot(normed_block, w_group, preferred_element_type=jnp.float32)
        summed = lax.psum_scatter(
            jnp.concatenate([first, second], axis=1), "grp", scatter_dimension=0, tiled=True
        )
        x_part = summed[:, :channels].astype(jnp.bfloat16)
        z_part = summed[:, channels : 2 * channels]
        b_mat = summed[:, 2 * channels : 2 * channels + state_dim]
        c_mat = summed[:, 2 * channels + state_dim : 2 * channels + 2 * state_dim]
        dt_all = summed[:, 2 * channels + 2 * state_dim :]
        dt_raw = lax.dynamic_slice_in_dim(dt_all, part_index * heads_dev, heads_dev, 1)
        taps = conv_weight[layer]
        window = conv_list[layer]
        conv_sum = x_part.astype(jnp.float32) * taps[taps_count - 1] + conv_bias[layer]
        for k in range(taps_count - 1):
            conv_sum = conv_sum + window[:, k].astype(jnp.float32) * taps[k]
        xc = jax.nn.silu(conv_sum)
        conv_list[layer] = jnp.concatenate([window[:, 1:], x_part[:, None, :]], axis=1)
        step_size = jax.nn.softplus(dt_raw + dt_bias[layer])
        decay = jnp.exp(-step_size * jnp.exp(a_log[layer]))
        xh = xc.reshape(row_dev, heads_dev, head_dim)
        fresh = (
            state_list[layer].astype(jnp.float32) * decay[:, :, None, None]
            + (step_size[:, :, None] * xh)[..., None] * b_mat[:, None, None, :]
        )
        state_list[layer] = fresh.astype(jnp.bfloat16)
        out_y = (
            jnp.sum(fresh * c_mat[:, None, None, :], axis=-1) + skip_gain[layer][None, :, None] * xh
        )
        gated = (out_y.reshape(row_dev, channels) * jax.nn.silu(z_part)).astype(jnp.bfloat16)
        w_back = out_weight[layer]
        partial_out = jnp.dot(
            lax.all_gather(gated, "grp", axis=0, tiled=True),
            w_back,
            preferred_element_type=jnp.float32,
        )
        return lax.psum(partial_out, "tp").astype(jnp.bfloat16)

    results = []
    for section in range(steps):
        carried = section > 0
        hidden = embeds[section]
        for layer in range(layers):
            if carried:
                migrate(layer)
            hf = hidden.astype(jnp.float32)
            normed = (
                hf * lax.rsqrt(jnp.mean(hf * hf, axis=-1, keepdims=True) + 1e-05) * norm_gain[layer]
            ).astype(jnp.bfloat16)
            normed_block = lax.all_to_all(normed, "grp", split_axis=1, concat_axis=0, tiled=True)
            delta = mixer(normed_block, layer)
            delta_rows = lax.all_to_all(delta, "grp", split_axis=0, concat_axis=1, tiled=True)
            hidden = (hf + delta_rows.astype(jnp.float32)).astype(jnp.bfloat16)
        results.append(lax.dynamic_slice_in_dim(hidden, part_index * part_width, part_width, 1))
    return jnp.stack(results)


def solution(mesh):
    placed = (
        P(None, "grp", None),
        P(None, "grp", "tp", None, None),
        P(None, "grp", None, "tp"),
        P(),
        P(None, "grp", None, "tp"),
        P(None, "grp", None),
        P(None, "tp"),
        P(None, "tp"),
        P(None, "tp"),
        P(None, None, "tp"),
        P(None, "tp"),
        P(None, "tp", "grp"),
        P("grp"),
        P("grp"),
    )
    return jax.shard_map(
        local, mesh=mesh, in_specs=placed, out_specs=P(None, "grp", "tp"), check_vma=False
    )
```

profile of v0, /device:TPU:7, one launch (start us, length us, event | category | flops | bytes accessed | tf_op | source)
XLA Modules:
  0.0 555.1 jit_solution(1863969251240788435)
XLA Ops:
  10.4 5.5 all-to-all-start.4
  16.0 14.3 %fusion.74 = (bf16[1,1024,2,2048]{3,2,1,0:T(2,128)(2,1)}, bf16[1,1024,2,2048]{3,2,1,0:T(2,128)(2,1)}) fusion(bf16[2,1024,2,2048]{3,2,1,0:T(2,128)(2,1)} %param.18), kind=kLoop, calls=%fused_computation.180 | loop fusion | bytes 33554432 | tf_op jit(solution)/shard_map/slice | solution.py:85
  30.3 12.1 %copy.33 = bf16[128,8,2,2048]{3,1,2,0:T(8,128)(2,1)} copy(bf16[128,8,2,2048]{3,2,1,0:T(2,128)(2,1)} %bitcast.216) | data formatting | bytes 16777216
  43.3 12.2 %copy.34 = bf16[128,8,2,2048]{3,1,2,0:T(8,128)(2,1)} copy(bf16[128,8,2,2048]{3,2,1,0:T(2,128)(2,1)} %bitcast.215) | data formatting | bytes 16777216
  56.7 5.1 all-to-all-start
  77.9 49.0 %all-reduce.13.cloned.1.call-done = f32[32,4480]{1,0:T(8,128)} async-done(((f32[32,4480]{1,0:T(8,128)}), f32[32,4480]{1,0:T(8,128)}) %all-reduce.13.cloned.1.call-update) | async-done | bytes 573456
  134.2 16.0 %all-gather.2 = bf16[8,4,2048]{2,1,0:T(4,128)(2,1)S(1)} all-gather(bf16[1,4,2048]{2,1,0:T(4,128)(2,1)S(1)} %fusion.62), channel_id=1, replica_groups=mesh['tp'=4,'grp'=8] {'grp'}, dimensions={0}, use_global_device_ids=true | all-gather | bytes 147456 | tf_op jit(solution)/shard_map/all_gather | solution.py:119
  154.0 12.4 %all-reduce.18 = bf16[32,1024]{1,0:T(8,128)(2,1)S(1)} all-reduce(f32[32,1024]{1,0:T(8,128)S(1)} %fusion.8), channel_id=1, replica_groups=mesh['tp'=4,'grp'=8] {'tp'}, use_global_device_ids=true, to_apply=%region_3.4 | all-reduce | flops 32768 | bytes 196608 | tf_op jit(solution)/shard_map/psum | solution.py:123
  167.1 7.0 %all-to-all-start.1 = ((bf16[8,4,1024]{2,1,0:T(4,128)(2,1)}), bf16[8,4,1024]{2,1,0:T(4,128)(2,1)S(1)}, u32[]{:S(2)}, u32[]{:S(2)}) async-start(bf16[8,4,1024]{2,1,0:T(4,128)(2,1)} %all_to_all.91), calls=%async_computation.1 | async-start | bytes 131072 | tf_op jit(solution)/shard_map/all_to_all | solution.py:138
  197.3 57.1 %all-reduce.17.cloned.1.call-done = (f32[32,4480]{1,0:T(8,128)}, f32[32,4480]{1,0:T(8,128)}) async-done(((f32[32,4480]{1,0:T(8,128)}, f32[32,4480]{1,0:T(8,128)}), (f32[32,4480]{1,0:T(8,128)}, f32[32,4480]{1,0:T(8,128)})) %all-reduce.17.cloned.1.call-update) | async-done | bytes 1146896
  265.8 17.0 %all-gather.1 = bf16[16,3,2048]{2,1,0:T(4,128)(2,1)S(1)} all-gather(bf16[2,3,2048]{2,1,0:T(4,128)(2,1)S(1)} %copy.29), channel_id=3, replica_groups=mesh['tp'=4,'grp'=8] {'grp'}, dimensions={0}, use_global_device_ids=true | all-gather | bytes 221184 | tf_op jit(solution)/shard_map/all_gather | solution.py:75
  285.5 61.7 %all-gather.8.cloned.1.call-done = bf16[16,32,64,128]{3,2,1,0:T(8,128)(2,1)} async-done(((bf16[2,32,64,128]{3,2,1,0:T(8,128)(2,1)}), bf16[16,32,64,128]{3,2,1,0:T(8,128)(2,1)}) %all-gather.8.cloned.1.call-update) | async-done | bytes 8388624 | tf_op jit(solution)/shard_map/all_gather | solution.py:74
  347.2 5.6 %select_reduce_fusion = bf16[2,32,64,128]{3,2,1,0:T(8,128)(2,1)S(1)} fusion(bf16[8,2,32,64,128]{4,3,2,1,0:T(8,128)(2,1)} %bitcast.217, pred[8]{0:T(512)(128)(4,1)S(1)} %iota_compare_fusion), kind=kLoop, calls=%fused_computation | loop fusion | flops 7864320 | bytes 9437192 | tf_op jit(solution)/shard_map/reduce_sum | solution.py:48
  357.7 14.1 %all-gather.4 = bf16[8,4,2048]{2,1,0:T(4,128)(2,1)S(1)} all-gather(bf16[1,4,2048]{2,1,0:T(4,128)(2,1)S(1)} %fusion.64), channel_id=1, replica_groups=mesh['tp'=4,'grp'=8] {'grp'}, dimensions={0}, use_global_device_ids=true | all-gather | bytes 147456 | tf_op jit(solution)/shard_map/all_gather | solution.py:119
  374.9 12.4 %all-reduce.19 = bf16[32,1024]{1,0:T(8,128)(2,1)S(1)} all-reduce(f32[32,1024]{1,0:T(8,128)S(1)} %fusion.6), channel_id=1, replica_groups=mesh['tp'=4,'grp'=8] {'tp'}, use_global_device_ids=true, to_apply=%region_13.14 | all-reduce | flops 32768 | bytes 196608 | tf_op jit(solution)/shard_map/psum | solution.py:123
  387.3 11.2 %all_to_all.116 = bf16[8,4,1024]{2,1,0:T(4,128)(2,1)S(1)} all-to-all(bf16[8,4,1024]{2,1,0:T(4,128)(2,1)S(1)} %all_to_all.101), channel_id=1, replica_groups=mesh['tp'=4,'grp'=8] {'grp'}, dimensions={0} | all-to-all | bytes 131072 | tf_op jit(solution)/shard_map/all_to_all | solution.py:138
  398.8 8.3 %all_to_all.117 = bf16[4,8,1024]{2,0,1:T(4,128)(2,1)S(1)} all-to-all(bf16[4,8,1024]{2,0,1:T(4,128)(2,1)S(1)} %multiply_convert_fusion), channel_id=1, replica_groups=mesh['tp'=4,'grp'=8] {'grp'}, dimensions={1} | all-to-all | bytes 131072 | tf_op jit(solution)/shard_map/all_to_all | solution.py:136
  407.4 5.1 fusion.85
  413.9 54.2 %all-reduce.15.cloned.1.call-done = f32[32,4480]{1,0:T(8,128)} async-done(((f32[32,4480]{1,0:T(8,128)}), f32[32,4480]{1,0:T(8,128)}) %all-reduce.15.cloned.1.call-update) | async-done | bytes 573456
  474.1 16.0 %all-gather.5 = bf16[8,4,2048]{2,1,0:T(4,128)(2,1)S(1)} all-gather(bf16[1,4,2048]{2,1,0:T(4,128)(2,1)S(1)} %get-tuple-element.64), channel_id=1, replica_groups=mesh['tp'=4,'grp'=8] {'grp'}, dimensions={0}, use_global_device_ids=true | all-gather | bytes 147456 | tf_op jit(solution)/shard_map/all_gather | solution.py:119
  493.2 14.0 %all-gather.3 = bf16[8,4,2048]{2,1,0:T(4,128)(2,1)S(1)} all-gather(bf16[1,4,2048]{2,1,0:T(4,128)(2,1)S(1)} %get-tuple-element.63), channel_id=1, replica_groups=mesh['tp'=4,'grp'=8] {'grp'}, dimensions={0}, use_global_device_ids=true | all-gather | bytes 147456 | tf_op jit(solution)/shard_map/all_gather | solution.py:119
  510.3 15.5 %all-reduce.20 = (bf16[32,1024]{1,0:T(8,128)(2,1)S(1)}, bf16[32,1024]{1,0:T(8,128)(2,1)S(1)}) all-reduce(f32[32,1024]{1,0:T(8,128)S(1)} %fusion.2, f32[32,1024]{1,0:T(8,128)S(1)} %fusion.4), channel_id=1, replica_groups=mesh['tp'=4,'grp'=8] {'tp'}, use_global_device_ids=true, to_apply=%region_17.18 | all-reduce | flops 65536 | bytes 393216 | tf_op jit(solution)/shard_map/psum | solution.py:123
  526.5 7.2 %all-to-all-start.7 = ((bf16[8,4,1024]{2,1,0:T(4,128)(2,1)}), bf16[8,4,1024]{2,1,0:T(4,128)(2,1)S(1)}, u32[]{:S(2)}, u32[]{:S(2)}) async-start(bf16[8,4,1024]{2,1,0:T(4,128)(2,1)} %all_to_all.106), calls=%async_computation.7 | async-start | bytes 131072 | tf_op jit(solution)/shard_map/all_to_all | solution.py:138
  542.9 5.0 all-to-all-done.3
  (170 shorter events, 101.5 us)
Async XLA Ops:
  10.4 46.3 %all-to-all-start.4 = ((bf16[4,8,1024]{2,0,1:T(4,128)(2,1)}), bf16[4,8,1024]{2,0,1:T(4,128)(2,1)S(1)}, u32[]{:S(2)}, u32[]{:S(2)}) async-start(bf16[4,8,1024]{2,0,1:T(4,128)(2,1)} %get-tuple-element.60), calls=%async_computation.4 | async-start | bytes 131072 | tf_op jit(solution)/shard_map/all_to_all | solution.py:136
  43.3 90.0 %copy-start.6 = (f32[2048]{0:T(1024)}, f32[2048]{0:T(1024)S(1)}, u32[]{:S(2)}) copy-start(f32[2048]{0:T(1024)S(1)} %mul.533) | copy-start | bytes 24580
  43.3 18.5 %copy-start.21 = (f32[2,32]{1,0:T(2,128)S(1)}, f32[2,32]{1,0:T(2,128)}, u32[]{:S(2)}) copy-start(f32[2,32]{1,0:T(2,128)} %param.20) | copy-start | bytes 772
  43.3 23.6 %copy-start.2 = (bf16[2,1024,384]{2,1,0:T(8,128)(2,1)S(1)}, bf16[2,1024,384]{2,1,0:T(8,128)(2,1)}, u32[]{:S(2)}) copy-start(bf16[2,1024,384]{2,1,0:T(8,128)(2,1)} %param.19) | copy-start | bytes 4718596
  56.7 10.2 %all-to-all-start = ((bf16[4,8,1024]{2,0,1:T(4,128)(2,1)}), bf16[4,8,1024]{2,0,1:T(4,128)(2,1)S(1)}, u32[]{:S(2)}, u32[]{:S(2)}) async-start(bf16[4,8,1024]{2,0,1:T(4,128)(2,1)} %get-tuple-element.59), calls=%async_computation | async-start | bytes 131072 | tf_op jit(solution)/shard_map/all_to_all | solution.py:136
  61.8 65.0 %all-reduce.13.cloned.1.call-start = ((), (), s32[]{:S(2)}) async-start(), calls=%async_computation.9 | async-start | bytes 1146880
  62.4 66.3 %copy-start.14 = (f32[32]{0:T(128)}, f32[32]{0:T(128)S(1)}, u32[]{:S(2)}) copy-start(f32[32]{0:T(128)S(1)} %get-tuple-element.70) | copy-start | bytes 388
  62.4 66.3 %copy-start.16 = (f32[32]{0:T(128)}, f32[32]{0:T(128)S(1)}, u32[]{:S(2)}) copy-start(f32[32]{0:T(128)S(1)} %get-tuple-element.73) | copy-start | bytes 388
  133.1 46.1 %copy-start.4 = (bf16[2,4,8192]{2,1,0:T(4,128)(2,1)S(1)}, bf16[2,4,8192]{2,1,0:T(4,128)(2,1)}, u32[]{:S(2)}) copy-start(bf16[2,4,8192]{2,1,0:T(4,128)(2,1)} %param.14) | copy-start | bytes 393220
  167.1 12.1 %all-to-all-start.1 = ((bf16[8,4,1024]{2,1,0:T(4,128)(2,1)}), bf16[8,4,1024]{2,1,0:T(4,128)(2,1)S(1)}, u32[]{:S(2)}, u32[]{:S(2)}) async-start(bf16[8,4,1024]{2,1,0:T(4,128)(2,1)} %all_to_all.91), calls=%async_computation.1 | async-start | bytes 131072 | tf_op jit(solution)/shard_map/all_to_all | solution.py:138
  180.2 9.2 %all-to-all-start.2 = ((bf16[4,8,1024]{2,0,1:T(4,128)(2,1)}), bf16[4,8,1024]{2,0,1:T(4,128)(2,1)S(1)}, u32[]{:S(2)}, u32[]{:S(2)}) async-start(bf16[4,8,1024]{2,0,1:T(4,128)(2,1)} %multiply_convert_fusion.2), calls=%async_computation.2 | async-start | bytes 131072 | tf_op jit(solution)/shard_map/all_to_all | solution.py:136
  184.3 70.1 %all-reduce.17.cloned.1.call-start = ((), (), s32[]{:S(2)}) async-start(), calls=%async_computation.11 | async-start | bytes 2293760
  190.8 65.5 %copy-start.10 = (f32[32]{0:T(128)S(1)}, f32[32]{0:T(128)}, u32[]{:S(2)}) copy-start(f32[32]{0:T(128)} %get-tuple-element.69) | copy-start | bytes 388
  190.8 65.5 %copy-start.12 = (f32[32]{0:T(128)S(1)}, f32[32]{0:T(128)}, u32[]{:S(2)}) copy-start(f32[32]{0:T(128)} %get-tuple-element.74) | copy-start | bytes 388
  196.6 150.6 %all-gather.8.cloned.1.call-start = ((), (), s32[]{:S(2)}) async-start(), calls=%async_computation.8 | async-start | bytes 9437184 | tf_op jit(solution)/shard_map/all_gather | solution.py:74
  256.4 28.9 %copy-start.15 = (f32[32]{0:T(128)S(1)}, f32[32]{0:T(128)}, u32[]{:S(2)}) copy-start(f32[32]{0:T(128)} %copy-done.14) | copy-start | bytes 388
  256.4 28.9 %copy-start.17 = (f32[32]{0:T(128)S(1)}, f32[32]{0:T(128)}, u32[]{:S(2)}) copy-start(f32[32]{0:T(128)} %copy-done.16) | copy-start | bytes 388
  263.1 205.0 %all-reduce.15.cloned.1.call-start = ((), (), s32[]{:S(2)}) async-start(), calls=%async_computation.10 | async-start | bytes 1146880
  356.5 50.6 %copy-start.3 = (bf16[2,1024,384]{2,1,0:T(8,128)(2,1)S(1)}, bf16[2,1024,384]{2,1,0:T(8,128)(2,1)}, u32[]{:S(2)}) copy-start(bf16[2,1024,384]{2,1,0:T(8,128)(2,1)} %param.19) | copy-start | bytes 4718596
  407.4 62.5 %copy-start.11 = (f32[32]{0:T(128)S(1)}, f32[32]{0:T(128)}, u32[]{:S(2)}) copy-start(f32[32]{0:T(128)} %get-tuple-element.69) | copy-start | bytes 388
  407.4 62.5 %copy-start.13 = (f32[32]{0:T(128)S(1)}, f32[32]{0:T(128)}, u32[]{:S(2)}) copy-start(f32[32]{0:T(128)} %get-tuple-element.74) | copy-start | bytes 388
  407.4 62.7 %copy-start.1 = (bf16[4,32,64,128]{3,2,1,0:T(8,128)(2,1)S(1)}, bf16[4,32,64,128]{3,2,1,0:T(8,128)(2,1)}, u32[]{:S(2)}) copy-start(bf16[4,32,64,128]{3,2,1,0:T(8,128)(2,1)} %get-tuple-element.31) | copy-start | bytes 6291460
  526.5 12.2 %all-to-all-start.7 = ((bf16[8,4,1024]{2,1,0:T(4,128)(2,1)}), bf16[8,4,1024]{2,1,0:T(4,128)(2,1)S(1)}, u32[]{:S(2)}, u32[]{:S(2)}) async-start(bf16[8,4,1024]{2,1,0:T(4,128)(2,1)} %all_to_all.106), calls=%async_computation.7 | async-start | bytes 131072 | tf_op jit(solution)/shard_map/all_to_all | solution.py:138
  538.7 9.2 %all-to-all-start.3 = ((bf16[8,4,1024]{2,1,0:T(4,128)(2,1)}), bf16[8,4,1024]{2,1,0:T(4,128)(2,1)S(1)}, u32[]{:S(2)}, u32[]{:S(2)}) async-start(bf16[8,4,1024]{2,1,0:T(4,128)(2,1)} %all_to_all.96), calls=%async_computation.3 | async-start | bytes 131072 | tf_op jit(solution)/shard_map/all_to_all | solution.py:138
  (9 other events, 90.7 us)
Sparse Core Ops, SparseCore 0:
  73.1 53.7 all-reduce.12
  196.7 57.6 all-reduce.16
  263.2 83.9 all-gather.7
  413.5 54.5 all-reduce.14
where the time goes:
time: 561 us; the launch traced here: 555 us
  waiting for transfers between devices  244 us (43%)
  blocking collectives  137 us (24%)
  local copies, waits for them, and re-layouts  53.6 us (10%)
  other arithmetic  36.8 us (7%)
  matrix products  35.1 us (6%)
  starting transfers between devices  33.1 us (6%)
  between operations  15.7 us (3%)
    unnamed x7, waiting for transfers between devices  160 us
    all_gather x1, waiting for transfers between devices, migrate_all(): lax.all_gather(own_state[None], 'grp', axis=0, tiled=True)  61.7 us
    all_gather x4, blocking collectives, mixer(): lax.all_gather(gated, 'grp', axis=0, tiled=True)  60.1 us
    psum x3, blocking collectives, mixer(): return lax.psum(partial_out, 'tp').astype(jnp.bfloat16)  40.4 us
    unnamed x53, local copies, waits for them, and re-layouts  27.1 us
    dot_general x4, matrix products, mixer(): first = jnp.dot(normed_block, w_cols, preferred_element_type=jnp.float32)  19.8 us
    all_to_all x3, starting transfers between devices, local(): lax.all_to_all(delta, 'grp', split_axis=0, concat_axis=1, tiled=True)  18.3 us
    all_gather x1, blocking collectives, migrate_all(): lax.all_gather(own_conv[None], 'grp', axis=0, tiled=True)  17 us
  transfers between devices with their start and end apart: 10, of which 9 were waited for; matrix products, arithmetic and copies ran while one was open for 10% of the time, Pallas kernels for 0%

commit v1 on v0

v1 whole, which is shorter than its diff:
```python
import functools

import jax
import jax.numpy as jnp
from jax import lax
from jax.experimental import pallas as pl
from jax.experimental.pallas import tpu as pltpu
from jax.sharding import PartitionSpec as P

F32 = jnp.float32
BF = jnp.bfloat16
LANES = 128


def iota(shape, dim):
    return lax.broadcasted_iota(jnp.int32, shape, dim)


def mm(a, b):
    return jnp.dot(a, b, preferred_element_type=F32)


def silu(v):
    return v / (1.0 + jnp.exp(-v))


def remote(src, dst, send_sem, recv_sem, axis, peer):
    return pltpu.make_async_remote_copy(
        src_ref=src,
        dst_ref=dst,
        send_sem=send_sem,
        recv_sem=recv_sem,
        device_id={axis: peer},
        device_id_type=pl.DeviceIdType.MESH,
    )


def kernel(
    groups, parts, heads_dev, head_dim, chunk_in, chunk_out,
    emb, conv, gain, head, taps, cbias, info, state, w_in, w_grp, w_out,
    out,
    win_v, wg_v, wout_v, st_v,
    emb_r, info_r, e32, info32, pre, sel, lhs, hxs,
    m_send, m_recv, a_send, a_recv, b_send, b_recv, c_send, c_recv, o_send, o_recv,
    hl, y8, xz, gat, o32, keep_d, keep_u, keep_x, keep_b,
    load_sem, es_sem, er_sem, is_sem, ir_sem, ms_sem, mr_sem, as_sem, ar_sem,
    bs_sem, br_sem, cs_sem, cr_sem, os_sem, or_sem,
):
    g = lax.axis_index("grp")
    t = lax.axis_index("tp")
    steps, row_dev, width = emb.shape
    layers = gain.shape[0]
    block = width // groups
    rows = groups * row_dev
    pair = 2 * row_dev
    channels = taps.shape[2]
    taps_count = taps.shape[1]
    state_dim = st_v.shape[3]
    mix_width = wg_v.shape[2]
    n_in = channels // chunk_in
    n_out = block // chunk_out
    share = groups // parts

    loads = []
    for l in range(layers):
        for i, (src, dst) in enumerate(
            ((w_grp, wg_v), (w_in, win_v), (state, st_v), (w_out, wout_v))
        ):
            cp = pltpu.make_async_copy(src.at[l], dst.at[l], load_sem.at[l, i])
            cp.start()
            loads.append(cp)

    barrier = pltpu.get_barrier_semaphore()
    for d in range(1, groups):
        pl.semaphore_signal(
            barrier, inc=1, device_id={"grp": lax.rem(g + d, groups)},
            device_id_type=pl.DeviceIdType.MESH,
        )
    for d in range(1, parts):
        pl.semaphore_signal(
            barrier, inc=1, device_id={"tp": lax.rem(t + d, parts)},
            device_id_type=pl.DeviceIdType.MESH,
        )
    pl.semaphore_wait(barrier, groups - 1 + parts - 1)

    def columns(who):
        return pl.ds(pl.multiple_of(who * block, block), block)

    first_sends = []
    for d in range(1, groups):
        peer = lax.rem(g + d, groups)
        cp = remote(emb.at[:, :, columns(peer)], emb_r.at[g], es_sem.at[d], er_sem.at[g], "grp", peer)
        cp.start()
        first_sends.append(cp)
        cp = remote(info, info_r.at[g], is_sem.at[d], ir_sem.at[g], "grp", peer)
        cp.start()
        first_sends.append(cp)
    emb_r[g] = emb[:, :, columns(g)]
    info_r[g] = info[...]

    for s in range(steps):
        for l in range(layers):
            total = jnp.zeros((row_dev, channels), F32)
            for k in range(taps_count - 1):
                if s + k <= taps_count - 2:
                    total = total + conv[l, s + k].astype(F32) * taps[l, k : k + 1, :]
            pre[s, l] = total + cbias[l : l + 1, :]
    n_heads = sel.shape[0]
    sel[...] = (
        iota((n_heads, channels), 0) == t * heads_dev + iota((n_heads, channels), 1) // head_dim
    ).astype(F32).astype(BF)
    dup_row = iota((2 * rows, rows), 0)
    dup = (
        iota((2 * rows, rows), 1) == (dup_row // pair) * row_dev + lax.rem(dup_row, row_dev)
    ).astype(F32).astype(BF)
    und_col = iota((rows, 2 * rows), 1)
    und_row = iota((rows, 2 * rows), 0)
    undup = (
        und_col == (und_row // row_dev) * pair + lax.rem(und_row, row_dev)
    ).astype(F32).astype(BF)
    spread = (
        iota((LANES, 2 * LANES), 1) // 2 == iota((LANES, 2 * LANES), 0)
    ).astype(F32).astype(BF)
    own_half = lax.rem(iota((2 * rows, 2 * LANES), 1), 2) == lax.rem(
        iota((2 * rows, 2 * LANES), 0) // row_dev, 2
    )

    for d in range(1, groups):
        src = lax.rem(g + groups - d, groups)
        remote(emb.at[:, :, columns(src)], emb_r.at[src], es_sem.at[d], er_sem.at[src], "grp", src).wait_recv()
        remote(info, info_r.at[src], is_sem.at[d], ir_sem.at[src], "grp", src).wait_recv()
    for i in range(groups):
        for s in range(steps):
            e32[s, i * row_dev : (i + 1) * row_dev, :] = emb_r[i, s].astype(F32)
        for q in range(2):
            info32[q, i * row_dev : (i + 1) * row_dev, :] = info_r[i, q]

    row_i = iota((rows, LANES), 0)
    col_i = iota((rows, LANES), 1)
    on_diag = row_i == col_i
    leave_of_row = info32[0]
    from_of_row = info32[1]
    leave_of_col = jnp.sum(jnp.where(on_diag, leave_of_row, 0.0), axis=0, keepdims=True)
    from_of_col = jnp.sum(jnp.where(on_diag, from_of_row, 0.0), axis=0, keepdims=True)
    slot_row = lax.rem(row_i, row_dev).astype(F32)
    slot_col = lax.rem(col_i, row_dev).astype(F32)
    group_row = (row_i // row_dev).astype(F32)
    group_col = (col_i // row_dev).astype(F32)
    diag = jnp.where(on_diag, 1.0, 0.0)
    hit = jnp.where(group_col == from_of_row, 1.0, 0.0) * jnp.where(slot_col == leave_of_col, 1.0, 0.0)
    to_slot = jnp.where(slot_row == leave_of_row, hit, diag)[:, :rows].astype(BF)
    hit_t = jnp.where(group_row == from_of_col, 1.0, 0.0) * jnp.where(slot_row == leave_of_row, 1.0, 0.0)
    to_home = jnp.where(slot_col == leave_of_col, hit_t, diag)[:, :rows].astype(BF)

    for cp in first_sends:
        cp.wait_send()

    out_sends = []
    for s in range(steps):
        start = e32[s].astype(BF)
        for _ in range(s):
            start = mm(to_home, start).astype(BF)
        hxs[...] = mm(dup, start)
        for l in range(layers):
            k = s * layers + l
            sends = []
            hx = hxs[...]
            gained = (hx * gain[l : l + 1, columns(g)]).astype(BF)
            if s == 0:
                loads[4 * l].wait()
            mix = mm(gained, wg_v[l])
            square = jnp.broadcast_to(jnp.sum(hx * hx, axis=1, keepdims=True), (2 * rows, LANES))
            for i in range(groups):
                m_send[i, :, :mix_width] = mix[i * pair : i * pair + row_dev]
                m_send[i, :, mix_width:] = square[i * pair : i * pair + row_dev]
            for d in range(1, groups):
                peer = lax.rem(g + d, groups)
                cp = remote(m_send.at[peer], m_recv.at[k, g], ms_sem.at[d], mr_sem.at[k, g], "grp", peer)
                cp.start()
                sends.append(cp)
            m_recv[k, g] = m_send[g]
            for j in range(block // LANES):
                wide = mm(gained[:, j * LANES : (j + 1) * LANES], spread)
                lhs[:, 2 * j * LANES : 2 * (j + 1) * LANES] = jnp.where(own_half, wide, 0.0).astype(BF)
            if s == 0:
                loads[4 * l + 1].wait()
            for c in range(n_in):
                acc = mm(lhs[...], win_v[l, :, c * chunk_in : (c + 1) * chunk_in])
                for i in range(groups):
                    a_send[c, i] = acc[i * pair : (i + 1) * pair].astype(BF)
                for d in range(1, groups):
                    peer = lax.rem(g + d, groups)
                    cp = remote(
                        a_send.at[c, peer], a_recv.at[k, c, g], as_sem.at[c, d], ar_sem.at[k, c, g], "grp", peer
                    )
                    cp.start()
                    sends.append(cp)
                a_recv[k, c, g] = a_send[c, g]

            for d in range(1, groups):
                src = lax.rem(g + groups - d, groups)
                remote(m_send.at[src], m_recv.at[k, src], ms_sem.at[d], mr_sem.at[k, src], "grp", src).wait_recv()
            msum = m_recv[k, 0]
            for i in range(1, groups):
                msum = msum + m_recv[k, i]
            scale = lax.rsqrt(msum[:, mix_width : mix_width + 1] / width + 1e-05)
            b_mat = msum[:, :state_dim] * scale
            c_mat = msum[:, state_dim : 2 * state_dim] * scale
            dt_all = msum[:, 2 * state_dim : mix_width] * scale
            keep_b[l, s] = b_mat
            dt_hi = dt_all.astype(BF)
            dt_lo = (dt_all - dt_hi.astype(F32)).astype(BF)
            dt_ch = mm(dt_hi, sel[...]) + mm(dt_lo, sel[...])
            pre_dt = dt_ch + head[0, l : l + 1, :]
            step_size = jnp.maximum(pre_dt, 0.0) + jnp.log1p(jnp.exp(-jnp.abs(pre_dt)))
            keep_d[l, s] = jnp.exp(-step_size * jnp.exp(head[1, l : l + 1, :]))
            c_hi = c_mat.astype(BF).astype(F32)
            hl[0:row_dev, :] = c_hi
            hl[row_dev:pair, :] = c_mat - c_hi
            c_both = hl[...].astype(BF)
            if s == 0:
                loads[4 * l + 2].wait()
            slot8 = lax.rem(iota((pair, channels), 0), row_dev)
            total = jnp.zeros((pair, channels), F32)
            for r in range(row_dev):
                got = lax.dot_general(
                    c_both, st_v[l, r], (((1,), (1,)), ((), ())), preferred_element_type=F32
                )
                total = jnp.where(slot8 == r, got, total)
            y8[...] = total
            acc_y = y8[0:row_dev, :] + y8[row_dev:pair, :]

            for c in range(n_in):
                for d in range(1, groups):
                    src = lax.rem(g + groups - d, groups)
                    remote(
                        a_send.at[c, src], a_recv.at[k, c, src], as_sem.at[c, d], ar_sem.at[k, c, src], "grp", src
                    ).wait_recv()
                asum = a_recv[k, c, 0].astype(F32)
                for i in range(1, groups):
                    asum = asum + a_recv[k, c, i].astype(F32)
                xz[:, c * chunk_in : (c + 1) * chunk_in] = asum
            x = (xz[0:row_dev, :] * scale).astype(BF).astype(F32)
            z = xz[row_dev:pair, :] * scale
            keep_x[l, s] = x
            conv_sum = pre[s, l] + x * taps[l, taps_count - 1 : taps_count, :]
            for e in range(s):
                tap = taps_count - 1 + e - s
                if tap >= 0:
                    conv_sum = conv_sum + keep_x[l, e] * taps[l, tap : tap + 1, :]
            xc = silu(conv_sum)
            keep_u[l, s] = step_size * xc
            for e in range(s + 1):
                bc = jnp.sum(keep_b[l, e] * c_mat, axis=1, keepdims=True)
                acc_y = keep_d[l, e] * acc_y + keep_u[l, e] * bc
            gated = ((acc_y + head[2, l : l + 1, :] * xc) * silu(z)).astype(BF)
            b_send[k] = gated
            b_recv[k, g] = gated
            for d in range(1, groups):
                peer = lax.rem(g + d, groups)
                cp = remote(b_send.at[k], b_recv.at[k, g], bs_sem.at[d], br_sem.at[k, g], "grp", peer)
                cp.start()
                sends.append(cp)
            for d in range(1, groups):
                src = lax.rem(g + groups - d, groups)
                remote(b_send.at[k], b_recv.at[k, src], bs_sem.at[d], br_sem.at[k, src], "grp", src).wait_recv()
            for i in range(groups):
                gat[i * row_dev : (i + 1) * row_dev, :] = b_recv[k, i].astype(F32)
            gated_all = gat[...].astype(BF)
            if s == 0:
                loads[4 * l + 3].wait()
            for c in range(n_out):
                part = mm(gated_all, wout_v[l, :, c * chunk_out : (c + 1) * chunk_out]).astype(BF)
                c_send[k, c] = part
                c_recv[k, c, t] = part
                for d in range(1, parts):
                    peer = lax.rem(t + d, parts)
                    cp = remote(
                        c_send.at[k, c], c_recv.at[k, c, t], cs_sem.at[c, d], cr_sem.at[k, c, t], "tp", peer
                    )
                    cp.start()
                    sends.append(cp)
            for c in range(n_out):
                for d in range(1, parts):
                    src = lax.rem(t + parts - d, parts)
                    remote(
                        c_send.at[k, c], c_recv.at[k, c, src], cs_sem.at[c, d], cr_sem.at[k, c, src], "tp", src
                    ).wait_recv()
                dsum = c_recv[k, c, 0].astype(F32)
                for i in range(1, parts):
                    dsum = dsum + c_recv[k, c, i].astype(F32)
                cols = slice(c * chunk_out, (c + 1) * chunk_out)
                hxs[:, cols] = (hxs[:, cols] + mm(dup, dsum.astype(BF))).astype(BF).astype(F32)
            for cp in sends:
                cp.wait_send()

        final = mm(undup, hxs[...].astype(BF))
        for _ in range(s):
            final = mm(to_slot, final.astype(BF))
        o32[...] = final
        for i in range(groups):
            o_send[s, i] = o32[i * row_dev : (i + 1) * row_dev, :].astype(BF)

        @pl.when(g // share == t)
        def _(s=s):
            for d in range(1, groups):
                peer = lax.rem(g + d, groups)
                remote(
                    o_send.at[s, peer], o_recv.at[s, lax.rem(g, share)], os_sem.at[s, d],
                    or_sem.at[s, lax.rem(g, share)], "grp", peer,
                ).start()
            o_recv[s, lax.rem(g, share)] = o_send[s, g]

    for s in range(steps):
        for j in range(share):
            src = t * share + j

            @pl.when(src != g)
            def _(s=s, j=j, src=src):
                remote(
                    o_send.at[s, src], o_recv.at[s, j], os_sem.at[s, 1], or_sem.at[s, j], "grp", src
                ).wait_recv()

            out[s, :, j * block : (j + 1) * block] = o_recv[s, j]

    @pl.when(g // share == t)
    def _():
        for s in range(steps):
            for d in range(1, groups):
                peer = lax.rem(g + d, groups)
                remote(
                    o_send.at[s, peer], o_recv.at[s, lax.rem(g, share)], os_sem.at[s, d],
                    or_sem.at[s, lax.rem(g, share)], "grp", peer,
                ).wait_send()


def local(
    embeds, ssm_state, conv_state, norm_gain, in_weight, group_weight, dt_bias, a_log,
    skip_gain, conv_weight, conv_bias, out_weight, leave_row, arrive_from,
):
    groups = lax.axis_size("grp")
    parts = lax.axis_size("tp")
    steps, row_dev, width = embeds.shape
    layers, _, heads_dev, head_dim, state_dim = ssm_state.shape
    block = in_weight.shape[1]
    channels = in_weight.shape[3]
    mix_width = group_weight.shape[2]
    n_heads = mix_width - 2 * state_dim
    rows = groups * row_dev
    pair = 2 * row_dev
    share = groups // parts
    rounds = steps * layers
    chunk_in = min(512, channels)
    chunk_out = min(512, block)
    n_in = channels // chunk_in
    n_out = block // chunk_out

    state = ssm_state.reshape(layers, row_dev, channels, state_dim)
    conv = conv_state.transpose(0, 2, 1, 3)
    w_in = in_weight.reshape(layers, 2 * block, channels)
    head = jnp.repeat(jnp.stack([dt_bias, a_log, skip_gain]), head_dim, axis=2)
    info = jnp.broadcast_to(
        jnp.concatenate([leave_row, arrive_from]).astype(F32)[:, None, None], (2, row_dev, LANES)
    )
    vm = pl.BlockSpec(memory_space=pltpu.VMEM)
    anywhere = pl.BlockSpec(memory_space=pl.ANY)
    dma = pltpu.SemaphoreType.DMA
    V = pltpu.VMEM
    return pl.pallas_call(
        functools.partial(kernel, groups, parts, heads_dev, head_dim, chunk_in, chunk_out),
        out_shape=jax.ShapeDtypeStruct((steps, row_dev, width // parts), BF),
        in_specs=[vm] * 7 + [anywhere] * 4,
        out_specs=vm,
        scratch_shapes=[
            V((layers, 2 * block, channels), BF),
            V((layers, block, mix_width), BF),
            V((layers, channels, block), BF),
            V((layers, row_dev, channels, state_dim), BF),
            V((groups, steps, row_dev, block), BF),
            V((groups, 2, row_dev, LANES), F32),
            V((steps, rows, block), F32),
            V((2, rows, LANES), F32),
            V((steps, layers, row_dev, channels), F32),
            V((n_heads, channels), BF),
            V((2 * rows, 2 * block), BF),
            V((2 * rows, block), F32),
            V((groups, row_dev, mix_width + LANES), F32),
            V((rounds, groups, row_dev, mix_width + LANES), F32),
            V((n_in, groups, pair, chunk_in), BF),
            V((rounds, n_in, groups, pair, chunk_in), BF),
            V((rounds, row_dev, channels), BF),
            V((rounds, groups, row_dev, channels), BF),
            V((rounds, n_out, rows, chunk_out), BF),
            V((rounds, n_out, parts, rows, chunk_out), BF),
            V((steps, groups, row_dev, block), BF),
            V((steps, share, row_dev, block), BF),
            V((pair, state_dim), F32),
            V((pair, channels), F32),
            V((pair, channels), F32),
            V((rows, channels), F32),
            V((rows, block), F32),
            V((layers, steps, row_dev, channels), F32),
            V((layers, steps, row_dev, channels), F32),
            V((layers, steps, row_dev, channels), F32),
            V((layers, steps, row_dev, state_dim), F32),
            dma((layers, 4)),
            dma((groups,)),
            dma((groups,)),
            dma((groups,)),
            dma((groups,)),
            dma((groups,)),
            dma((rounds, groups)),
            dma((n_in, groups)),
            dma((rounds, n_in, groups)),
            dma((groups,)),
            dma((rounds, groups)),
            dma((n_out, parts)),
            dma((rounds, n_out, parts)),
            dma((steps, groups)),
            dma((steps, share)),
        ],
        compiler_params=pltpu.CompilerParams(
            collective_id=0, has_side_effects=True, vmem_limit_bytes=60 * 2**20
        ),
    )(embeds, conv, norm_gain, head, conv_weight, conv_bias, info, state, w_in, group_weight, out_weight)


def solution(mesh):
    placed = (
        P(None, "grp", None),
        P(None, "grp", "tp", None, None),
        P(None, "grp", None, "tp"),
        P(),
        P(None, "grp", None, "tp"),
        P(None, "grp", None),
        P(None, "tp"),
        P(None, "tp"),
        P(None, "tp"),
        P(None, None, "tp"),
        P(None, "tp"),
        P(None, "tp", "grp"),
        P("grp"),
        P("grp"),
    )
    return jax.shard_map(
        local, mesh=mesh, in_specs=placed, out_specs=P(None, "grp", "tp"), check_vma=False
    )
```

time: 561 us -> 126 us (0.22)
  waiting for transfers between devices: 244 us -> 0 us
  blocking collectives: 137 us -> 0 us
  Pallas kernels: 0 us -> 94.8 us
  other arithmetic: 36.8 us -> 0.79 us
  matrix products: 35.1 us -> 0 us
  starting transfers between devices: 33.1 us -> 0 us
  local copies, waits for them, and re-layouts: 53.6 us -> 27.7 us
  between operations: 15.7 us -> 1.32 us
    unnamed x7 -> x0, waiting for transfers between devices: 160 us -> none
    pallas_call x0 -> x1, Pallas kernels: none -> 94.8 us  [local(): pl.pallas_call(functools.partial(kernel, groups, parts, heads_dev, head_d...]
    all_gather x5 -> x0, blocking collectives: 77.2 us -> none  [the longest x4 60.1 us: mixer(): lax.all_gather(gated, 'grp', axis=0, tiled=True)]
    all_gather x1 -> x0, waiting for transfers between devices: 61.7 us -> none  [migrate_all(): lax.all_gather(own_state[None], 'grp', axis=0, tiled=True)]
    psum x3 -> x0, blocking collectives: 40.4 us -> none  [mixer(): return lax.psum(partial_out, 'tp').astype(jnp.bfloat16)]
    dot_general x12 -> x0, matrix products: 35.1 us -> none  [the longest x4 19.8 us: mixer(): first = jnp.dot(normed_block, w_cols, preferred_element_type=jnp.float32)]
    all_to_all x6 -> x0, starting transfers between devices: 33 us -> none  [the longest x3 18.3 us: local(): lax.all_to_all(delta, 'grp', split_axis=0, concat_axis=1, tiled=True)]
    unnamed x53 -> x1, local copies, waits for them, and re-layouts: 27.1 us -> 1.39 us
  transfers between devices with their start and end apart: 10 -> 0, of which waited for: 9 -> 0; matrix products, arithmetic and copies ran while one was open for 10% -> 0% of each run, Pallas kernels for 0% -> 0%
where the time goes in v1:
time: 126 us; the launch traced here: 125 us
  Pallas kernels  94.8 us (75%)
  local copies, waits for them, and re-layouts  27.7 us (22%)
  between operations  1.32 us (1%)
    pallas_call x1, Pallas kernels, local(): pl.pallas_call(functools.partial(kernel, groups, parts, heads_dev, head_d...  94.8 us
    reshape x1, local copies, waits for them, and re-layouts, local(): w_in = in_weight.reshape(layers, 2 * block, channels)  24.9 us

profile of v1, /device:TPU:7, one launch (start us, length us, event | category | flops | bytes accessed | tf_op | source)
XLA Modules:
  0.0 124.7 jit_solution(13142839030195536118)
XLA Ops:
  1.3 0.1 add_convert_fusion
  1.4 0.7 pad_maximum_fusion
  2.1 0.7 broadcast_in_dim.10.info
  2.8 0.1 broadcast_in_dim.4
  2.8 0.7 reshape.24.head
  3.6 24.9 %reshape.26.w_in = bf16[2,2048,2048]{2,1,0:T(8,128)(2,1)} reshape(bf16[2,1024,2,2048]{3,2,1,0:T(2,128)(2,1)} %param.18) | data formatting | bytes 33554432 | tf_op jit(solution)/shard_map/reshape | solution.py:360
  28.4 94.8 %shard_map.136 = bf16[2,4,2048]{2,1,0:T(4,128)(2,1)} custom-call(bf16[2,4,8192]{2,1,0:T(4,128)(2,1)} %emb.1, bf16[2,3,4,2048]{3,2,1,0:T(4,128)(2,1)} %bitcast.8, f32[2,8192]{1,0:T(2,128)} %gain.1, f32[3,2,2048]{2,1,0:T(2,128)} %reshape.24.head, f32[2,4,2048]{2,1,0:T(4,128)} %taps.1, f32[2,2048]{1,0:T(2,128)} %cbias.1, f32[2,4,128]{2,1,0:T(4,128)} %broadcast_in_dim.10.info, ...), custom_call_target="tpu_custom_call" | custom-call | tf_op jit(solution)/shard_map/pallas_call | solution.py:369
  123.3 1.4 %copy.18 = bf16[2,4,2048]{2,1,0:T(4,128)(2,1)} copy(bf16[2,4,2048]{2,1,0:T(4,128)(2,1)} %shard_map.136) | data formatting | bytes 65536

commit v2 on v1

--- a/solution.py
+++ b/solution.py
@@ -37,13 +37,14 @@
 
 def kernel(
     groups, parts, heads_dev, head_dim, chunk_in, chunk_out,
-    emb, conv, gain, head, taps, cbias, info, state, w_in, w_grp, w_out,
+    emb, conv, gain, dt_bias, a_log, skip, taps, cbias, leave, arrive, state, w_in, w_grp, w_out,
     out,
     win_v, wg_v, wout_v, st_v,
     emb_r, info_r, e32, info32, pre, sel, lhs, hxs,
-    m_send, m_recv, a_send, a_recv, b_send, b_recv, c_send, c_recv, o_send, o_recv,
+    head, info, m_send, m_pair, m_z, m_recv, a_send, a_pair, a_z, a_recv, b_send, b_recv, c_send, c_recv, o_send, o_recv,
     hl, y8, xz, gat, o32, keep_d, keep_u, keep_x, keep_b,
-    load_sem, es_sem, er_sem, is_sem, ir_sem, ms_sem, mr_sem, as_sem, ar_sem,
+    load_sem, in_sem, es_sem, er_sem, is_sem, ir_sem, mps_sem, mpr_sem, ms_sem, mr_sem,
+    aps_sem, apr_sem, as_sem, ar_sem,
     bs_sem, br_sem, cs_sem, cr_sem, os_sem, or_sem,
 ):
     g = lax.axis_index("grp")
@@ -60,15 +61,26 @@
     n_in = channels // chunk_in
     n_out = block // chunk_out
     share = groups // parts
-
-    loads = []
+    half = groups // 2
+    core = lax.rem(g, 2)
+    chip = g // 2
+    partner = g + 1 - 2 * core
+    n_tiles = channels // LANES
+    tiles_in = chunk_in // LANES
+
+    loads = {}
     for l in range(layers):
-        for i, (src, dst) in enumerate(
-            ((w_grp, wg_v), (w_in, win_v), (state, st_v), (w_out, wout_v))
-        ):
-            cp = pltpu.make_async_copy(src.at[l], dst.at[l], load_sem.at[l, i])
-            cp.start()
-            loads.append(cp)
+        plan = [("grp", w_grp.at[l], wg_v.at[l], load_sem.at[l, 0])]
+        for n in range(n_tiles):
+            tile = slice(n * LANES, (n + 1) * LANES)
+            plan.append((n, w_in.at[l, :, :, tile], win_v.at[l, n], in_sem.at[l, n]))
+        plan.append(("state", state.at[l], st_v.at[l], load_sem.at[l, 1]))
+        plan.append(("out", w_out.at[l], wout_v.at[l], load_sem.at[l, 2]))
+        for name, src, dst, sem in plan:
+            loads[l, name] = pltpu.make_async_copy(src, dst, sem)
+            loads[l, name].start()
+    info[0] = jnp.full((row_dev, LANES), leave[0].astype(F32), F32)
+    info[1] = jnp.full((row_dev, LANES), arrive[0].astype(F32), F32)
 
     barrier = pltpu.get_barrier_semaphore()
     for d in range(1, groups):
@@ -109,6 +121,17 @@
     sel[...] = (
         iota((n_heads, channels), 0) == t * heads_dev + iota((n_heads, channels), 1) // head_dim
     ).astype(F32).astype(BF)
+    own_head = (
+        iota((heads_dev, channels), 1) // head_dim == iota((heads_dev, channels), 0)
+    ).astype(F32).astype(BF)
+    for i, param in enumerate((dt_bias, a_log, skip)):
+        rest = param[...]
+        wide = jnp.zeros((layers, channels), F32)
+        for _ in range(3):
+            piece = rest.astype(BF)
+            rest = rest - piece.astype(F32)
+            wide = wide + mm(piece, own_head)
+        head[i] = wide
     dup_row = iota((2 * rows, rows), 0)
     dup = (
         iota((2 * rows, rows), 1) == (dup_row // pair) * row_dev + lax.rem(dup_row, row_dev)
@@ -167,41 +190,67 @@
             hx = hxs[...]
             gained = (hx * gain[l : l + 1, columns(g)]).astype(BF)
             if s == 0:
-                loads[4 * l].wait()
+                loads[l, "grp"].wait()
             mix = mm(gained, wg_v[l])
             square = jnp.broadcast_to(jnp.sum(hx * hx, axis=1, keepdims=True), (2 * rows, LANES))
             for i in range(groups):
-                m_send[i, :, :mix_width] = mix[i * pair : i * pair + row_dev]
-                m_send[i, :, mix_width:] = square[i * pair : i * pair + row_dev]
-            for d in range(1, groups):
-                peer = lax.rem(g + d, groups)
-                cp = remote(m_send.at[peer], m_recv.at[k, g], ms_sem.at[d], mr_sem.at[k, g], "grp", peer)
-                cp.start()
-                sends.append(cp)
-            m_recv[k, g] = m_send[g]
+                m_send[i % 2, i // 2, :, :mix_width] = mix[i * pair : i * pair + row_dev]
+                m_send[i % 2, i // 2, :, mix_width:] = square[i * pair : i * pair + row_dev]
+            m_cross = remote(m_send.at[1 - core], m_pair.at[k], mps_sem.at[0], mpr_sem.at[k], "grp", partner)
+            m_cross.start()
+            sends.append(m_cross)
             for j in range(block // LANES):
                 wide = mm(gained[:, j * LANES : (j + 1) * LANES], spread)
                 lhs[:, 2 * j * LANES : 2 * (j + 1) * LANES] = jnp.where(own_half, wide, 0.0).astype(BF)
-            if s == 0:
-                loads[4 * l + 1].wait()
-            for c in range(n_in):
-                acc = mm(lhs[...], win_v[l, :, c * chunk_in : (c + 1) * chunk_in])
-                for i in range(groups):
-                    a_send[c, i] = acc[i * pair : (i + 1) * pair].astype(BF)
-                for d in range(1, groups):
-                    peer = lax.rem(g + d, groups)
-                    cp = remote(
-                        a_send.at[c, peer], a_recv.at[k, c, g], as_sem.at[c, d], ar_sem.at[k, c, g], "grp", peer
+            crossing = []
+            for c in range(n_in + 1):
+                if c < n_in:
+                    tiles = []
+                    for n in range(c * tiles_in, (c + 1) * tiles_in):
+                        if s == 0:
+                            loads[l, n].wait()
+                        tiles.append(win_v[l, n].reshape(2 * block, LANES))
+                    acc = mm(lhs[...], jnp.concatenate(tiles, axis=1))
+                    for i in range(groups):
+                        a_send[c, i % 2, i // 2] = acc[i * pair : (i + 1) * pair].astype(BF)
+                    cross = remote(
+                        a_send.at[c, 1 - core], a_pair.at[k, c], aps_sem.at[c], apr_sem.at[k, c], "grp", partner
                     )
-                    cp.start()
-                    sends.append(cp)
-                a_recv[k, c, g] = a_send[c, g]
-
-            for d in range(1, groups):
-                src = lax.rem(g + groups - d, groups)
-                remote(m_send.at[src], m_recv.at[k, src], ms_sem.at[d], mr_sem.at[k, src], "grp", src).wait_recv()
+                    cross.start()
+                    sends.append(cross)
+                    crossing.append(cross)
+                if c == 0:
+                    m_cross.wait_recv()
+                    m_z[...] = m_send[core] + m_pair[k]
+                    for d in range(1, half):
+                        to = lax.rem(chip + d, half)
+                        cp = remote(
+                            m_z.at[to], m_recv.at[k, chip], ms_sem.at[d], mr_sem.at[k, chip], "grp", 2 * to + core
+                        )
+                        cp.start()
+                        sends.append(cp)
+                    m_recv[k, chip] = m_z[chip]
+                else:
+                    e = c - 1
+                    crossing[e].wait_recv()
+                    a_z[e] = (a_send[e, core].astype(F32) + a_pair[k, e].astype(F32)).astype(BF)
+                    for d in range(1, half):
+                        to = lax.rem(chip + d, half)
+                        cp = remote(
+                            a_z.at[e, to], a_recv.at[k, e, chip], as_sem.at[e, d], ar_sem.at[k, e, chip],
+                            "grp", 2 * to + core,
+                        )
+                        cp.start()
+                        sends.append(cp)
+                    a_recv[k, e, chip] = a_z[e, chip]
+
+            for d in range(1, half):
+                src = lax.rem(chip + half - d, half)
+                remote(
+                    m_z.at[src], m_recv.at[k, src], ms_sem.at[d], mr_sem.at[k, src], "grp", 2 * src + core
+                ).wait_recv()
             msum = m_recv[k, 0]
-            for i in range(1, groups):
+            for i in range(1, half):
                 msum = msum + m_recv[k, i]
             scale = lax.rsqrt(msum[:, mix_width : mix_width + 1] / width + 1e-05)
             b_mat = msum[:, :state_dim] * scale
@@ -219,7 +268,7 @@
             hl[row_dev:pair, :] = c_mat - c_hi
             c_both = hl[...].astype(BF)
             if s == 0:
-                loads[4 * l + 2].wait()
+                loads[l, "state"].wait()
             slot8 = lax.rem(iota((pair, channels), 0), row_dev)
             total = jnp.zeros((pair, channels), F32)
             for r in range(row_dev):
@@ -231,13 +280,14 @@
             acc_y = y8[0:row_dev, :] + y8[row_dev:pair, :]
 
             for c in range(n_in):
-                for d in range(1, groups):
-                    src = lax.rem(g + groups - d, groups)
+                for d in range(1, half):
+                    src = lax.rem(chip + half - d, half)
                     remote(
-                        a_send.at[c, src], a_recv.at[k, c, src], as_sem.at[c, d], ar_sem.at[k, c, src], "grp", src
+                        a_z.at[c, src], a_recv.at[k, c, src], as_sem.at[c, d], ar_sem.at[k, c, src],
+                        "grp", 2 * src + core,
                     ).wait_recv()
                 asum = a_recv[k, c, 0].astype(F32)
-                for i in range(1, groups):
+                for i in range(1, half):
                     asum = asum + a_recv[k, c, i].astype(F32)
                 xz[:, c * chunk_in : (c + 1) * chunk_in] = asum
             x = (xz[0:row_dev, :] * scale).astype(BF).astype(F32)
@@ -268,7 +318,7 @@
                 gat[i * row_dev : (i + 1) * row_dev, :] = b_recv[k, i].astype(F32)
             gated_all = gat[...].astype(BF)
             if s == 0:
-                loads[4 * l + 3].wait()
+                loads[l, "out"].wait()
             for c in range(n_out):
                 part = mm(gated_all, wout_v[l, :, c * chunk_out : (c + 1) * chunk_out]).astype(BF)
                 c_send[k, c] = part
@@ -349,6 +399,7 @@
     rows = groups * row_dev
     pair = 2 * row_dev
     share = groups // parts
+    half = groups // 2
     rounds = steps * layers
     chunk_in = min(512, channels)
     chunk_out = min(512, block)
@@ -357,11 +408,6 @@
 
     state = ssm_state.reshape(layers, row_dev, channels, state_dim)
     conv = conv_state.transpose(0, 2, 1, 3)
-    w_in = in_weight.reshape(layers, 2 * block, channels)
-    head = jnp.repeat(jnp.stack([dt_bias, a_log, skip_gain]), head_dim, axis=2)
-    info = jnp.broadcast_to(
-        jnp.concatenate([leave_row, arrive_from]).astype(F32)[:, None, None], (2, row_dev, LANES)
-    )
     vm = pl.BlockSpec(memory_space=pltpu.VMEM)
     anywhere = pl.BlockSpec(memory_space=pl.ANY)
     dma = pltpu.SemaphoreType.DMA
@@ -369,10 +415,10 @@
     return pl.pallas_call(
         functools.partial(kernel, groups, parts, heads_dev, head_dim, chunk_in, chunk_out),
         out_shape=jax.ShapeDtypeStruct((steps, row_dev, width // parts), BF),
-        in_specs=[vm] * 7 + [anywhere] * 4,
+        in_specs=[vm] * 8 + [pl.BlockSpec(memory_space=pltpu.SMEM)] * 2 + [anywhere] * 4,
         out_specs=vm,
         scratch_shapes=[
-            V((layers, 2 * block, channels), BF),
+            V((layers, channels // LANES, block, 2, LANES), BF),
             V((layers, block, mix_width), BF),
             V((layers, channels, block), BF),
             V((layers, row_dev, channels, state_dim), BF),
@@ -384,10 +430,16 @@
             V((n_heads, channels), BF),
             V((2 * rows, 2 * block), BF),
             V((2 * rows, block), F32),
-            V((groups, row_dev, mix_width + LANES), F32),
-            V((rounds, groups, row_dev, mix_width + LANES), F32),
-            V((n_in, groups, pair, chunk_in), BF),
-            V((rounds, n_in, groups, pair, chunk_in), BF),
+            V((3, layers, channels), F32),
+            V((2, row_dev, LANES), F32),
+            V((2, half, row_dev, mix_width + LANES), F32),
+            V((rounds, half, row_dev, mix_width + LANES), F32),
+            V((half, row_dev, mix_width + LANES), F32),
+            V((rounds, half, row_dev, mix_width + LANES), F32),
+            V((n_in, 2, half, pair, chunk_in), BF),
+            V((rounds, n_in, half, pair, chunk_in), BF),
+            V((n_in, half, pair, chunk_in), BF),
+            V((rounds, n_in, half, pair, chunk_in), BF),
             V((rounds, row_dev, channels), BF),
             V((rounds, groups, row_dev, channels), BF),
             V((rounds, n_out, rows, chunk_out), BF),
@@ -403,15 +455,20 @@
             V((layers, steps, row_dev, channels), F32),
             V((layers, steps, row_dev, channels), F32),
             V((layers, steps, row_dev, state_dim), F32),
-            dma((layers, 4)),
+            dma((layers, 3)),
+            dma((layers, channels // LANES)),
             dma((groups,)),
             dma((groups,)),
             dma((groups,)),
             dma((groups,)),
-            dma((groups,)),
-            dma((rounds, groups)),
-            dma((n_in, groups)),
-            dma((rounds, n_in, groups)),
+            dma((1,)),
+            dma((rounds,)),
+            dma((half,)),
+            dma((rounds, half)),
+            dma((n_in,)),
+            dma((rounds, n_in)),
+            dma((n_in, half)),
+            dma((rounds, n_in, half)),
             dma((groups,)),
             dma((rounds, groups)),
             dma((n_out, parts)),
@@ -422,7 +479,10 @@
         compiler_params=pltpu.CompilerParams(
             collective_id=0, has_side_effects=True, vmem_limit_bytes=60 * 2**20
         ),
-    )(embeds, conv, norm_gain, head, conv_weight, conv_bias, info, state, w_in, group_weight, out_weight)
+    )(
+        embeds, conv, norm_gain, dt_bias, a_log, skip_gain, conv_weight, conv_bias, leave_row, arrive_from,
+        state, in_weight, group_weight, out_weight,
+    )
 
 
 def solution(mesh):

time: 126 us -> 105 us (0.83)
  local copies, waits for them, and re-layouts: 27.7 us -> 1.39 us
  Pallas kernels: 94.8 us -> 102 us
    reshape x2 -> x0, local copies, waits for them, and re-layouts: 25.6 us -> none  [the longest x1 24.9 us: local(): w_in = in_weight.reshape(layers, 2 * block, channels)]
    pallas_call x1, Pallas kernels: 94.8 us -> 102 us  [local(): pl.pallas_call(functools.partial(kernel, groups, parts, heads_dev, head_d...]
where the time goes in v2:
time: 105 us
  Pallas kernels  102 us (97%)
  local copies, waits for them, and re-layouts  1.39 us (1%)
  between operations  1.31 us (1%)
    pallas_call x1, Pallas kernels, local(): pl.pallas_call(functools.partial(kernel, groups, parts, heads_dev, head_d...  102 us

profile of v2, /device:TPU:7, one launch (start us, length us, event | category | flops | bytes accessed | tf_op | source)
XLA Modules:
  0.0 104.8 jit_solution(7238208035325371397)
XLA Ops:
  1.3 102.1 %shard_map.136 = bf16[2,4,2048]{2,1,0:T(4,128)(2,1)} custom-call(bf16[2,4,8192]{2,1,0:T(4,128)(2,1)} %emb.1, bf16[2,3,4,2048]{3,2,1,0:T(4,128)(2,1)} %bitcast.3, f32[2,8192]{1,0:T(2,128)} %gain.1, f32[2,32]{1,0:T(2,128)} %dt_bias.1, f32[2,32]{1,0:T(2,128)} %a_log.1, f32[2,32]{1,0:T(2,128)} %skip.1, f32[2,4,2048]{2,1,0:T(4,128)} %taps.1, f32[2,2048]{1,0:T(2,128)} %cbias.1, ...), custom_call_target="tpu_custom_call" | custom-call | tf_op jit(solution)/shard_map/pallas_call | solution.py:415
  103.4 1.4 %copy.18 = bf16[2,4,2048]{2,1,0:T(4,128)(2,1)} copy(bf16[2,4,2048]{2,1,0:T(4,128)(2,1)} %shard_map.136) | data formatting | bytes 65536
